TPU v7x, 128 devices: a whole 4x4x4 slice. The times are simulated.
128 devices in a mesh: section: 4 (over x), tensor: 32 (over z, y, core).
Axes of the slice: x: 4, y: 4, z: 4, core: 2. Of those that a mesh axis runs over, the one named last changes fastest.
Arguments:
- inputs: bfloat16 [4, 1024, 8192], P('section', None, 'tensor'), may hold values from -6 to 6
- preact: bfloat16 [4, 1024, 32768], P('section', None, 'tensor'), may hold values from -6 to 6
- handoff: bfloat16 [4, 1024, 8192], P('section', None, 'tensor'), may hold values from -6 to 6
- first_blocks: bfloat16 [4, 128, 6, 256, 256], P('section', 'tensor'), may hold values from -0.15625 to 0.15625
- second_blocks: bfloat16 [4, 128, 6, 256, 256], P('section', 'tensor'), may hold values from -0.078125 to 0.078125
- left_one: bfloat16 [4, 8192, 256], P('section', 'tensor'), may hold values from -0.0625 to 0.0625
- right_one: bfloat16 [4, 256, 32768], P('section', None, 'tensor'), may hold values from -0.375 to 0.375
- left_two: bfloat16 [4, 32768, 256], P('section', 'tensor'), may hold values from -0.03125 to 0.03125
- right_two: bfloat16 [4, 256, 8192], P('section', None, 'tensor'), may hold values from -0.375 to 0.375
Outputs:
- input_grad: bfloat16 [4, 1024, 8192], P('section', None, 'tensor')
- first_grad: bfloat16 [4, 128, 6, 256, 256], P('section', 'tensor')
- second_grad: bfloat16 [4, 128, 6, 256, 256], P('section', 'tensor')
- leftone_grad: bfloat16 [4, 8192, 256], P('section', 'tensor')
- rightone_grad: bfloat16 [4, 256, 32768], P('section', None, 'tensor')
- lefttwo_grad: bfloat16 [4, 32768, 256], P('section', 'tensor')
- righttwo_grad: bfloat16 [4, 256, 8192], P('section', None, 'tensor')
All inputs are finite; a program needn't handle non-finite values.
Results may differ from a plain program's by a relative error of at most 0.0061.
Values may be sent and summed in bfloat16 or wider, within the bound.
A program may use at most 128 MiB of HBM per device.

v0:
```python
import jax
import jax.numpy as jnp
from jax import lax
from jax.sharding import PartitionSpec as P


def swapped(value, axis, apart):
    mask = 2**apart
    pairs = [(source, source ^ mask) for source in range(lax.axis_size(axis))]
    return lax.ppermute(value, axis, pairs)


def shifted(shard, axis, by):
    peers = lax.axis_size(axis)
    return lax.ppermute(shard, axis, [(i, (i + by) % peers) for i in range(peers)])


def gelu_pair(preact):
    values = preact.astype(jnp.float32)
    normal_cdf = 0.5 * (1.0 + jax.scipy.special.erf(values * 0.7071067811865476))
    density = jnp.exp(-0.5 * values * values) * 0.3989422804014327
    return (values * normal_cdf, normal_cdf + values * density)


def partner_sets(values, count_in, link_count, swapper):
    local_bits = count_in.bit_length() - 1
    result = [values]
    for degree in range(1, link_count):
        result.append(swapper(values, degree - 1 - local_bits))
    return result


def body(
    inputs, preact, handoff, first_blocks, second_blocks, left_one, right_one, left_two, right_two
):
    own_inputs = inputs[0]
    blocks_one = first_blocks[0]
    blocks_two = second_blocks[0]
    hid_count = blocks_one.shape[0]
    link_count = blocks_one.shape[1]
    block_size = blocks_one.shape[-1]
    row_count = own_inputs.shape[0]
    feat_width = own_inputs.shape[1]
    count_in = feat_width // block_size
    group_size = hid_count // count_in
    local_bits = count_in.bit_length() - 1
    activated, slope_vals = gelu_pair(preact[0])
    activated = activated.astype(jnp.bfloat16)
    proj_in, proj_act = lax.psum(
        (
            jnp.dot(own_inputs, left_one[0], preferred_element_type=jnp.float32),
            jnp.dot(activated, left_two[0], preferred_element_type=jnp.float32),
        ),
        "tensor",
    )
    proj_in = proj_in.astype(jnp.bfloat16)
    proj_act = proj_act.astype(jnp.bfloat16)

    def swap_inputs(values, bit_pos):
        return swapped(values, "tensor", bit_pos)

    def swap_grads(values, bit_pos):
        return swapped(values, "tensor", bit_pos)

    input_sets = jnp.stack(partner_sets(own_inputs, count_in, link_count, swap_inputs))
    upstream = shifted(handoff[0], "section", -1)
    grad_sets = jnp.stack(partner_sets(upstream, count_in, link_count, swap_grads))
    proj_grad = lax.psum(
        jnp.dot(upstream, right_two[0].T, preferred_element_type=jnp.float32), "tensor"
    ).astype(jnp.bfloat16)
    grad_view = grad_sets.reshape(link_count, row_count, count_in, block_size)
    second_view = blocks_two.reshape(count_in, group_size, link_count, block_size, block_size)
    grad_act = jnp.einsum(
        "ktcb,cjkeb->tcje", grad_view, second_view, preferred_element_type=jnp.float32
    ).reshape(row_count, hid_count * block_size)
    grad_act = grad_act + jnp.dot(proj_grad, left_two[0].T, preferred_element_type=jnp.float32)
    hidden_grad = (grad_act * slope_vals).astype(jnp.bfloat16)
    back_rank = lax.psum(
        jnp.dot(hidden_grad, right_one[0].T, preferred_element_type=jnp.float32), "tensor"
    ).astype(jnp.bfloat16)
    hidden_view = hidden_grad.reshape(row_count, count_in, group_size, block_size)
    first_view = blocks_one.reshape(count_in, group_size, link_count, block_size, block_size)
    partials = jnp.einsum(
        "tcje,cjkbe->ktcb", hidden_view, first_view, preferred_element_type=jnp.float32
    ).reshape(link_count, row_count, feat_width)
    summed_grad = partials[0] + jnp.dot(
        back_rank, left_one[0].T, preferred_element_type=jnp.float32
    )
    degree_order = list(range(1, link_count))
    for degree in degree_order:
        summed_grad = summed_grad + swapped(partials[degree], "tensor", degree - 1 - local_bits)
    input_grad = summed_grad.astype(jnp.bfloat16)[None]
    input_view = input_sets.reshape(link_count, row_count, count_in, block_size)
    first_grad = jnp.einsum(
        "ktcb,tcje->cjkbe", input_view, hidden_view, preferred_element_type=jnp.float32
    )
    first_grad = first_grad.reshape(hid_count, link_count, block_size, block_size).astype(
        jnp.bfloat16
    )[None]
    activ_view = activated.reshape(row_count, count_in, group_size, block_size)
    second_grad = jnp.einsum(
        "tcje,ktcb->cjkeb", activ_view, grad_view, preferred_element_type=jnp.float32
    )
    second_grad = second_grad.reshape(hid_count, link_count, block_size, block_size).astype(
        jnp.bfloat16
    )[None]
    leftone_grad = jnp.dot(own_inputs.T, back_rank, preferred_element_type=jnp.float32).astype(
        jnp.bfloat16
    )[None]
    rightone_grad = jnp.dot(proj_in.T, hidden_grad, preferred_element_type=jnp.float32).astype(
        jnp.bfloat16
    )[None]
    lefttwo_grad = jnp.dot(activated.T, proj_grad, preferred_element_type=jnp.float32).astype(
        jnp.bfloat16
    )[None]
    righttwo_grad = jnp.dot(proj_act.T, upstream, preferred_element_type=jnp.float32).astype(
        jnp.bfloat16
    )[None]
    return (
        input_grad,
        first_grad,
        second_grad,
        leftone_grad,
        rightone_grad,
        lefttwo_grad,
        righttwo_grad,
    )


def solution(mesh):
    in_specs = (
        P("section", None, "tensor"),
        P("section", None, "tensor"),
        P("section", None, "tensor"),
        P("section", "tensor", None, None, None),
        P("section", "tensor", None, None, None),
        P("section", "tensor", None),
        P("section", None, "tensor"),
        P("section", "tensor", None),
        P("section", None, "tensor"),
    )
    out_specs = (
        P("section", None, "tensor"),
        P("section", "tensor", None, None, None),
        P("section", "tensor", None, None, None),
        P("section", "tensor", None),
        P("section", None, "tensor"),
        P("section", "tensor", None),
        P("section", None, "tensor"),
    )
    return jax.shard_map(body, mesh=mesh, in_specs=in_specs, out_specs=out_specs, check_vma=False)
```

profile of v0, /device:TPU:24, one launch (start us, length us, event | category | flops | bytes accessed | tf_op | source)
XLA Modules:
  0.0 437.4 jit_solution(17502697164771448957)
XLA Ops:
  0.7 4.0 collective-permute-start.15
  4.6 1.0 collective-permute-start.14
  5.6 1.2 collective-permute-start.13
  6.9 2.8 collective-permute-start
  9.6 3.9 copy.16
  13.6 2.3 fusion.17
  15.9 2.7 fusion.64
  18.6 1.8 fusion.33
  20.4 1.9 constant_dynamic-update-slice_fusion
  22.3 2.3 fusion.67
  24.6 122.4 %all-reduce.3 = bf16[1024,256]{1,0:T(8,128)(2,1)} all-reduce(f32[1024,256]{1,0:T(8,128)} %fusion.67), channel_id=1, replica_groups=mesh['section'=4,'tensor'=32] {'tensor'}, use_global_device_ids=true, to_apply=%region_0.0 | all-reduce | flops 262144 | bytes 1572864 | tf_op jit(solution)/shard_map/psum | solution.py:68
  147.0 3.7 fusion.45
  150.7 1.1 bitcast_dynamic-update-slice_fusion.10
  151.8 0.1 collective-permute-start.5
  151.9 1.1 bitcast_dynamic-update-slice_fusion.4
  153.0 14.0 %collective-permute-start.4 = (bf16[1024,256]{1,0:T(8,128)(2,1)}, bf16[1024,256]{1,0:T(8,128)(2,1)S(1)}, u32[]{:S(2)}, u32[]{:S(2)}) collective-permute-start(bf16[1024,256]{1,0:T(8,128)(2,1)} %collective-permute-done), channel_id=1, source_target_pairs={{0,8},{1,9},{2,10},{3,11},{4,12},{5,13},{6,14},{7,15},{8,0},{9,1},... | collective-permute-start | bytes 1572872 | tf_op jit(solution)/shard_map/ppermute | solution.py:10
  167.0 1.1 bitcast_dynamic-update-slice_fusion.3
  168.1 0.3 collective-permute-start.1
  168.3 1.1 bitcast_dynamic-update-slice_fusion.2
  169.4 0.1 collective-permute-start.2
  169.5 1.1 bitcast_dynamic-update-slice_fusion.1
  170.6 3.7 collective-permute-start.3
  174.4 1.1 bitcast_dynamic-update-slice_fusion
  175.5 9.0 %collective-permute-done.2 = bf16[1024,256]{1,0:T(8,128)(2,1)S(1)} collective-permute-done((bf16[1024,256]{1,0:T(8,128)(2,1)}, bf16[1024,256]{1,0:T(8,128)(2,1)S(1)}, u32[]{:S(2)}, u32[]{:S(2)}) %collective-permute-start.2) | collective-permute-done | bytes 524320 | tf_op jit(solution)/shard_map/ppermute | solution.py:10
  184.6 12.2 %collective-permute-done.3 = bf16[1024,256]{1,0:T(8,128)(2,1)S(1)} collective-permute-done((bf16[1024,256]{1,0:T(8,128)(2,1)}, bf16[1024,256]{1,0:T(8,128)(2,1)S(1)}, u32[]{:S(2)}, u32[]{:S(2)}) %collective-permute-start.3) | collective-permute-done | bytes 524320 | tf_op jit(solution)/shard_map/ppermute | solution.py:10
  196.9 1.7 copy-done.13
  198.6 4.9 %convert_bitcast_fusion.1 = bf16[1,4,6,256,256]{3,4,1,2,0:T(8,128)(2,1)} fusion(bf16[1024,4,256,1]{0,2,1,3:T(8,128)(2,1)S(1)} %bitcast.207, bf16[6,1024,256]{2,1,0:T(8,128)(2,1)S(1)} %bitcast_dynamic-update-slice_fusion.5), kind=kOutput, calls=%fused_computation.31 | convolution fusion | flops 3222798336 | bytes 8388608 | tf_op jit(solution)/shard_map/tcje,ktcb->cjkeb/dot_general | solution.py:101
  203.5 4.6 %copy.27 = bf16[1,4,6,256,256]{4,3,2,1,0:T(8,128)(2,1)} copy(bf16[1,4,6,256,256]{3,4,1,2,0:T(8,128)(2,1)} %convert_bitcast_fusion.1) | data formatting | bytes 6291456
  208.1 6.4 %fusion.24 = f32[1024,4,256,1]{0,2,3,1:T(8,128)S(1)} fusion(bf16[1,4,6,256,256]{4,3,2,1,0:T(8,128)(2,1)} %param.13, bf16[6,1024,256]{2,1,0:T(8,128)(2,1)} %copy-done.13), kind=kOutput, calls=%fused_computation.28 | convolution fusion | flops 3221225472 | bytes 10485760 | tf_op jit(solution)/shard_map/ktcb,cjkeb->tcje/dot_general | solution.py:73
  214.6 2.4 fusion.12
  217.0 1.3 copy-done.4
  218.4 1.7 fusion.51
  220.1 136.6 %all-reduce.4 = (bf16[1024,256]{1,0:T(8,128)(2,1)}, bf16[1024,256]{1,0:T(8,128)(2,1)}, bf16[1024,256]{1,0:T(8,128)(2,1)}) all-reduce(f32[1024,256]{1,0:T(8,128)} %fusion.51, f32[1024,256]{1,0:T(8,128)} %fusion.64, f32[1024,256]{1,0:T(8,128)} %fusion.33), channel_id=1, replica_groups=mesh['section'=4,'tensor'=32] {'tensor'}, use_global_device_ids=true, to_apply=%region_1.0 | all-reduce | flops 786432 | bytes 4718592 | tf_op jit(solution)/shard_map/psum | solution.py:78
  356.7 1.5 fusion.49
  358.2 0.8 copy.28
  359.0 5.1 %fusion.22 = f32[1024,6,256,1]{2,0,1,3:T(8,128)S(1)} fusion(bf16[1024,4,256,1]{0,2,3,1:T(8,128)(2,1)} %bitcast.205, bf16[1,4,6,256,256]{4,3,2,1,0:T(8,128)(2,1)S(1)} %copy-done), kind=kOutput, calls=%fused_computation.26 | convolution fusion | flops 3221225472 | bytes 11534336 | tf_op jit(solution)/shard_map/tcje,cjkbe->ktcb/dot_general | solution.py:83
  364.0 1.2 slice_bitcast_fusion
  365.2 2.1 slice_bitcast_fusion.4
  367.3 1.8 copy-done.3
  369.1 13.6 %collective-permute-start.9 = (f32[1024,256]{1,0:T(8,128)}, f32[1024,256]{1,0:T(8,128)}, u32[]{:S(2)}, u32[]{:S(2)}) collective-permute-start(f32[1024,256]{1,0:T(8,128)} %get-tuple-element.18), channel_id=1, source_target_pairs={{0,8},{1,9},{2,10},{3,11},{4,12},{5,13},{6,14},{7,15},{8,0},{9,1},... | collective-permute-start | bytes 3145736 | tf_op jit(solution)/shard_map/ppermute | solution.py:10
  382.7 4.3 collective-permute-start.7
  387.0 4.9 %convert_bitcast_fusion.2 = bf16[1,4,6,256,256]{3,4,2,1,0:T(8,128)(2,1)} fusion(bf16[1024,4,256,1]{0,2,3,1:T(8,128)(2,1)S(1)} %bitcast.206, bf16[6,1024,256]{2,1,0:T(8,128)(2,1)S(1)} %copy-done.16), kind=kOutput, calls=%fused_computation.32 | convolution fusion | flops 3222798336 | bytes 8388608 | tf_op jit(solution)/shard_map/ktcb,tcje->cjkbe/dot_general | solution.py:94
  391.9 4.7 %copy.26 = bf16[1,4,6,256,256]{4,3,2,1,0:T(8,128)(2,1)} copy(bf16[1,4,6,256,256]{3,4,2,1,0:T(8,128)(2,1)} %convert_bitcast_fusion.2) | data formatting | bytes 6291456
  396.6 2.1 fusion.50
  398.7 3.4 fusion.44
  402.1 24.5 %collective-permute-done.9 = f32[1024,256]{1,0:T(8,128)} collective-permute-done((f32[1024,256]{1,0:T(8,128)}, f32[1024,256]{1,0:T(8,128)}, u32[]{:S(2)}, u32[]{:S(2)}) %collective-permute-start.9) | collective-permute-done | bytes 1048608 | tf_op jit(solution)/shard_map/ppermute | solution.py:10
  426.6 6.7 %collective-permute-done.7 = f32[1024,256]{1,0:T(8,128)} collective-permute-done((f32[1024,256]{1,0:T(8,128)}, f32[1024,256]{1,0:T(8,128)}, u32[]{:S(2)}, u32[]{:S(2)}) %collective-permute-start.7) | collective-permute-done | bytes 1048608 | tf_op jit(solution)/shard_map/ppermute | solution.py:10
  433.3 4.1 fusion.48
  (59 shorter events, 0.3 us)
Async XLA Ops:
  0.6 358.3 %copy-start = (bf16[1,4,6,256,256]{4,3,2,1,0:T(8,128)(2,1)S(1)}, bf16[1,4,6,256,256]{4,3,2,1,0:T(8,128)(2,1)}, u32[]{:S(2)}) copy-start(bf16[1,4,6,256,256]{4,3,2,1,0:T(8,128)(2,1)} %param.12) | copy-start | bytes 9437188
  0.7 170.0 %collective-permute-start.15 = (bf16[1024,256]{1,0:T(8,128)(2,1)}, bf16[1024,256]{1,0:T(8,128)(2,1)}, u32[]{:S(2)}, u32[]{:S(2)}) collective-permute-start(bf16[1024,256]{1,0:T(8,128)(2,1)} %bitcast.45), channel_id=1, source_target_pairs={{0,16},{1,17},{2,18},{3,19},{4,20},{5,21},{6,22},{7,23},{8,24},{9,... | collective-permute-start | bytes 1572872 | tf_op jit(solution)/shard_map/ppermute | solution.py:10
  4.6 164.8 %collective-permute-start.14 = (bf16[1024,256]{1,0:T(8,128)(2,1)}, bf16[1024,256]{1,0:T(8,128)(2,1)}, u32[]{:S(2)}, u32[]{:S(2)}) collective-permute-start(bf16[1024,256]{1,0:T(8,128)(2,1)} %bitcast.45), channel_id=1, source_target_pairs={{0,8},{1,9},{2,10},{3,11},{4,12},{5,13},{6,14},{7,15},{8,0},{9,1},... | collective-permute-start | bytes 1572872 | tf_op jit(solution)/shard_map/ppermute | solution.py:10
  5.6 162.4 %collective-permute-start.13 = (bf16[1024,256]{1,0:T(8,128)(2,1)}, bf16[1024,256]{1,0:T(8,128)(2,1)}, u32[]{:S(2)}, u32[]{:S(2)}) collective-permute-start(bf16[1024,256]{1,0:T(8,128)(2,1)} %bitcast.45), channel_id=1, source_target_pairs={{0,4},{1,5},{2,6},{3,7},{4,0},{5,1},{6,2},{7,3},{8,12},{9,13},{10,... | collective-permute-start | bytes 1572872 | tf_op jit(solution)/shard_map/ppermute | solution.py:10
  6.9 146.1 %collective-permute-start.12 = (bf16[1024,256]{1,0:T(8,128)(2,1)}, bf16[1024,256]{1,0:T(8,128)(2,1)}, u32[]{:S(2)}, u32[]{:S(2)}) collective-permute-start(bf16[1024,256]{1,0:T(8,128)(2,1)} %bitcast.45), channel_id=1, source_target_pairs={{0,2},{1,3},{2,0},{3,1},{4,6},{5,7},{6,4},{7,5},{8,10},{9,11},{10,... | collective-permute-start | bytes 1572872 | tf_op jit(solution)/shard_map/ppermute | solution.py:10
  6.9 9.0 %copy-start.9 = (bf16[1,256,256]{2,1,0:T(8,128)(2,1)S(1)}, bf16[1,256,256]{2,1,0:T(8,128)(2,1)}, u32[]{:S(2)}) copy-start(bf16[1,256,256]{2,1,0:T(8,128)(2,1)} %param.14) | copy-start | bytes 393220
  6.9 15.4 %collective-permute-start = (bf16[1024,256]{1,0:T(8,128)(2,1)}, bf16[1024,256]{1,0:T(8,128)(2,1)}, u32[]{:S(2)}, u32[]{:S(2)}) collective-permute-start(bf16[1024,256]{1,0:T(8,128)(2,1)} %bitcast.208), channel_id=1, source_target_pairs={{0,96},{32,0},{64,32},{96,64},{1,97},{33,1},{65,33},{97,65},{2,98}... | collective-permute-start | bytes 1572872 | tf_op jit(solution)/shard_map/ppermute | solution.py:15
  13.6 5.1 %copy-start.17 = (bf16[1,1024,256]{2,1,0:T(8,128)(2,1)S(1)}, bf16[1,1024,256]{2,1,0:T(8,128)(2,1)}, u32[]{:S(2)}) copy-start(bf16[1,1024,256]{2,1,0:T(8,128)(2,1)} %param.16) | copy-start | bytes 1572868
  15.9 4.5 %copy-start.6 = (bf16[1,1024,1024]{1,2,0:T(8,128)(2,1)}, bf16[1,1024,1024]{1,2,0:T(8,128)(2,1)S(1)}, u32[]{:S(2)}) copy-start(bf16[1,1024,1024]{1,2,0:T(8,128)(2,1)S(1)} %fusion.17) | copy-start | bytes 6291460
  18.6 3.6 copy-start.12
  22.3 129.5 %collective-permute-start.11 = (bf16[1024,256]{1,0:T(8,128)(2,1)}, bf16[1024,256]{1,0:T(8,128)(2,1)}, u32[]{:S(2)}, u32[]{:S(2)}) collective-permute-start(bf16[1024,256]{1,0:T(8,128)(2,1)} %bitcast.45), channel_id=1, source_target_pairs={{0,1},{1,0},{2,3},{3,2},{4,5},{5,4},{6,7},{7,6},{8,9},{9,8},{10,11... | collective-permute-start | bytes 1572872 | tf_op jit(solution)/shard_map/ppermute | solution.py:10
  147.0 4.9 %copy-start.14 = (bf16[6,1024,256]{2,1,0:T(8,128)(2,1)S(1)}, bf16[6,1024,256]{2,1,0:T(8,128)(2,1)}, u32[]{:S(2)}) copy-start(bf16[6,1024,256]{2,1,0:T(8,128)(2,1)} %constant_dynamic-update-slice_fusion) | copy-start | bytes 9437188
  151.8 45.1 %collective-permute-start.5 = (bf16[1024,256]{1,0:T(8,128)(2,1)}, bf16[1024,256]{1,0:T(8,128)(2,1)S(1)}, u32[]{:S(2)}, u32[]{:S(2)}) collective-permute-start(bf16[1024,256]{1,0:T(8,128)(2,1)} %collective-permute-done), channel_id=1, source_target_pairs={{0,16},{1,17},{2,18},{3,19},{4,20},{5,21},{6,22},{7,23},{8,24},{9,... | collective-permute-start | bytes 1572872 | tf_op jit(solution)/shard_map/ppermute | solution.py:10
  153.0 43.8 %collective-permute-start.4 = (bf16[1024,256]{1,0:T(8,128)(2,1)}, bf16[1024,256]{1,0:T(8,128)(2,1)S(1)}, u32[]{:S(2)}, u32[]{:S(2)}) collective-permute-start(bf16[1024,256]{1,0:T(8,128)(2,1)} %collective-permute-done), channel_id=1, source_target_pairs={{0,8},{1,9},{2,10},{3,11},{4,12},{5,13},{6,14},{7,15},{8,0},{9,1},... | collective-permute-start | bytes 1572872 | tf_op jit(solution)/shard_map/ppermute | solution.py:10
  168.1 7.4 %collective-permute-start.1 = (bf16[1024,256]{1,0:T(8,128)(2,1)}, bf16[1024,256]{1,0:T(8,128)(2,1)S(1)}, u32[]{:S(2)}, u32[]{:S(2)}) collective-permute-start(bf16[1024,256]{1,0:T(8,128)(2,1)} %collective-permute-done), channel_id=1, source_target_pairs={{0,1},{1,0},{2,3},{3,2},{4,5},{5,4},{6,7},{7,6},{8,9},{9,8},{10,11... | collective-permute-start | bytes 1572872 | tf_op jit(solution)/shard_map/ppermute | solution.py:10
  169.4 15.1 %collective-permute-start.2 = (bf16[1024,256]{1,0:T(8,128)(2,1)}, bf16[1024,256]{1,0:T(8,128)(2,1)S(1)}, u32[]{:S(2)}, u32[]{:S(2)}) collective-permute-start(bf16[1024,256]{1,0:T(8,128)(2,1)} %collective-permute-done), channel_id=1, source_target_pairs={{0,2},{1,3},{2,0},{3,1},{4,6},{5,7},{6,4},{7,5},{8,10},{9,11},{10,... | collective-permute-start | bytes 1572872 | tf_op jit(solution)/shard_map/ppermute | solution.py:10
  170.6 28.0 %copy-start.7 = (bf16[1,1024,1024]{1,2,0:T(8,128)(2,1)S(1)}, bf16[1,1024,1024]{1,2,0:T(8,128)(2,1)}, u32[]{:S(2)}) copy-start(bf16[1,1024,1024]{1,2,0:T(8,128)(2,1)} %copy-done.6) | copy-start | bytes 6291460
  170.6 26.1 %collective-permute-start.3 = (bf16[1024,256]{1,0:T(8,128)(2,1)}, bf16[1024,256]{1,0:T(8,128)(2,1)S(1)}, u32[]{:S(2)}, u32[]{:S(2)}) collective-permute-start(bf16[1024,256]{1,0:T(8,128)(2,1)} %collective-permute-done), channel_id=1, source_target_pairs={{0,4},{1,5},{2,6},{3,7},{4,0},{5,1},{6,2},{7,3},{8,12},{9,13},{10,... | collective-permute-start | bytes 1572872 | tf_op jit(solution)/shard_map/ppermute | solution.py:10
  175.4 21.5 %copy-start.15 = (bf16[6,1024,256]{2,1,0:T(8,128)(2,1)}, bf16[6,1024,256]{2,1,0:T(8,128)(2,1)S(1)}, u32[]{:S(2)}) copy-start(bf16[6,1024,256]{2,1,0:T(8,128)(2,1)S(1)} %bitcast_dynamic-update-slice_fusion) | copy-start | bytes 9437188
  196.9 1.7 copy-start.13
  208.1 6.4 %copy-start.2 = (bf16[1,1024,1024]{1,2,0:T(8,128)(2,1)S(1)}, bf16[1,1024,1024]{1,2,0:T(8,128)(2,1)}, u32[]{:S(2)}) copy-start(bf16[1,1024,1024]{1,2,0:T(8,128)(2,1)} %copy.16) | copy-start | bytes 6291460
  208.1 6.4 %copy-start.11 = (bf16[1024,256]{1,0:T(8,128)(2,1)S(1)}, bf16[1024,256]{1,0:T(8,128)(2,1)}, u32[]{:S(2)}) copy-start(bf16[1024,256]{1,0:T(8,128)(2,1)} %all-reduce.3) | copy-start | bytes 1572868
  208.1 6.5 %copy-start.18 = (bf16[1,1024,256]{2,1,0:T(8,128)(2,1)S(1)}, bf16[1,1024,256]{2,1,0:T(8,128)(2,1)}, u32[]{:S(2)}) copy-start(bf16[1,1024,256]{2,1,0:T(8,128)(2,1)} %param.16) | copy-start | bytes 1572868
  214.6 3.8 copy-start.10
  217.0 1.3 copy-start.4
  364.0 5.1 %copy-start.3 = (f32[1024,6,256,1]{2,0,1,3:T(8,128)}, f32[1024,6,256,1]{2,0,1,3:T(8,128)S(1)}, u32[]{:S(2)}) copy-start(f32[1024,6,256,1]{2,0,1,3:T(8,128)S(1)} %fusion.22) | copy-start | bytes 18874372
  365.2 36.9 %collective-permute-start.10 = (f32[1024,256]{1,0:T(8,128)}, f32[1024,256]{1,0:T(8,128)}, u32[]{:S(2)}, u32[]{:S(2)}) collective-permute-start(f32[1024,256]{1,0:T(8,128)} %slice_bitcast_fusion), channel_id=1, source_target_pairs={{0,16},{1,17},{2,18},{3,19},{4,20},{5,21},{6,22},{7,23},{8,24},{9,... | collective-permute-start | bytes 3145736 | tf_op jit(solution)/shard_map/ppermute | solution.py:10
  365.2 21.7 %copy-start.5 = (bf16[1024,1024]{0,1:T(8,128)(2,1)S(1)}, bf16[1024,1024]{0,1:T(8,128)(2,1)}, u32[]{:S(2)}) copy-start(bf16[1024,1024]{0,1:T(8,128)(2,1)} %copy-done.4) | copy-start | bytes 6291460
  365.2 21.7 %copy-start.16 = (bf16[6,1024,256]{2,1,0:T(8,128)(2,1)S(1)}, bf16[6,1024,256]{2,1,0:T(8,128)(2,1)}, u32[]{:S(2)}) copy-start(bf16[6,1024,256]{2,1,0:T(8,128)(2,1)} %copy-done.15) | copy-start | bytes 9437188
  369.1 33.0 %collective-permute-start.6 = (f32[1024,256]{1,0:T(8,128)}, f32[1024,256]{1,0:T(8,128)}, u32[]{:S(2)}, u32[]{:S(2)}) collective-permute-start(f32[1024,256]{1,0:T(8,128)} %get-tuple-element.17), channel_id=1, source_target_pairs={{0,1},{1,0},{2,3},{3,2},{4,5},{5,4},{6,7},{7,6},{8,9},{9,8},{10,11... | collective-permute-start | bytes 3145736 | tf_op jit(solution)/shard_map/ppermute | solution.py:10
  369.1 57.5 %collective-permute-start.9 = (f32[1024,256]{1,0:T(8,128)}, f32[1024,256]{1,0:T(8,128)}, u32[]{:S(2)}, u32[]{:S(2)}) collective-permute-start(f32[1024,256]{1,0:T(8,128)} %get-tuple-element.18), channel_id=1, source_target_pairs={{0,8},{1,9},{2,10},{3,11},{4,12},{5,13},{6,14},{7,15},{8,0},{9,1},... | collective-permute-start | bytes 3145736 | tf_op jit(solution)/shard_map/ppermute | solution.py:10
  382.7 43.9 %collective-permute-start.8 = (f32[1024,256]{1,0:T(8,128)}, f32[1024,256]{1,0:T(8,128)}, u32[]{:S(2)}, u32[]{:S(2)}) collective-permute-start(f32[1024,256]{1,0:T(8,128)} %get-tuple-element.19), channel_id=1, source_target_pairs={{0,4},{1,5},{2,6},{3,7},{4,0},{5,1},{6,2},{7,3},{8,12},{9,13},{10,... | collective-permute-start | bytes 3145736 | tf_op jit(solution)/shard_map/ppermute | solution.py:10
  382.7 50.6 %collective-permute-start.7 = (f32[1024,256]{1,0:T(8,128)}, f32[1024,256]{1,0:T(8,128)}, u32[]{:S(2)}, u32[]{:S(2)}) collective-permute-start(f32[1024,256]{1,0:T(8,128)} %get-tuple-element.20), channel_id=1, source_target_pairs={{0,2},{1,3},{2,0},{3,1},{4,6},{5,7},{6,4},{7,5},{8,10},{9,11},{10,... | collective-permute-start | bytes 3145736 | tf_op jit(solution)/shard_map/ppermute | solution.py:10
  391.9 4.7 %copy-start.19 = (bf16[1024,256]{1,0:T(8,128)(2,1)S(1)}, bf16[1024,256]{1,0:T(8,128)(2,1)}, u32[]{:S(2)}) copy-start(bf16[1024,256]{1,0:T(8,128)(2,1)} %get-tuple-element.16) | copy-start | bytes 1572868
  396.5 36.8 %copy-start.8 = (bf16[1024,256]{1,0:T(8,128)(2,1)S(1)}, bf16[1024,256]{1,0:T(8,128)(2,1)}, u32[]{:S(2)}) copy-start(bf16[1024,256]{1,0:T(8,128)(2,1)} %get-tuple-element.14) | copy-start | bytes 1572868
  398.7 38.7 %copy-start.1 = (bf16[1,4,6,256,256]{4,3,2,1,0:T(8,128)(2,1)S(1)}, bf16[1,4,6,256,256]{4,3,2,1,0:T(8,128)(2,1)}, u32[]{:S(2)}) copy-start(bf16[1,4,6,256,256]{4,3,2,1,0:T(8,128)(2,1)} %param.12) | copy-start | bytes 9437188
where the time goes:
time: 438 us; the launch traced here: 437 us
  blocking collectives  259 us (59%)
  waiting for transfers between devices  52.4 us (12%)
  matrix products  47.2 us (11%)
  starting transfers between devices  45 us (10%)
  local copies, waits for them, and re-layouts  30.6 us (7%)
    psum x1, blocking collectives, body(): lax.psum(jnp.dot(hidden_grad, right_one[0].T, preferred_element_type=jnp....  137 us
    psum x1, blocking collectives, body(): lax.psum(jnp.dot(upstream, right_two[0].T, preferred_element_type=jnp.flo...  122 us
    ppermute x15, waiting for transfers between devices, swapped(): return lax.ppermute(value, axis, pairs)  52.4 us
    ppermute x15, starting transfers between devices, swapped(): return lax.ppermute(value, axis, pairs)  42.3 us
    unnamed x54, local copies, waits for them, and re-layouts  26.3 us
  transfers between devices with their start and end apart: 16, of which 4 were waited for; matrix products, arithmetic and copies ran while one was open for 10% of the time, Pallas kernels for 0%

commit v1 on v0

--- a/solution.py
+++ b/solution.py
@@ -65,8 +65,11 @@
     input_sets = jnp.stack(partner_sets(own_inputs, count_in, link_count, swap_inputs))
     upstream = shifted(handoff[0], "section", -1)
     grad_sets = jnp.stack(partner_sets(upstream, count_in, link_count, swap_grads))
-    proj_grad = lax.psum(
-        jnp.dot(upstream, right_two[0].T, preferred_element_type=jnp.float32), "tensor"
+    proj_grad = jnp.sum(
+        lax.all_gather(
+            jnp.dot(upstream, right_two[0].T, preferred_element_type=jnp.float32), "tensor"
+        ),
+        axis=0,
     ).astype(jnp.bfloat16)
     grad_view = grad_sets.reshape(link_count, row_count, count_in, block_size)
     second_view = blocks_two.reshape(count_in, group_size, link_count, block_size, block_size)

time: 438 us -> 417 us (0.952)
  the two profiles are of different devices: /device:TPU:24 before, /device:TPU:6 now
where the time goes in v1:
time: 417 us
  blocking collectives  184 us (44%)
  waiting for transfers between devices  112 us (27%)
  matrix products  46.7 us (11%)
  local copies, waits for them, and re-layouts  27.7 us (7%)
  starting transfers between devices  16.9 us (4%)
  other arithmetic  15.2 us (4%)
  between operations  14.3 us (3%)
    psum x1, blocking collectives, body(): lax.psum(jnp.dot(hidden_grad, right_one[0].T, preferred_element_type=jnp....  184 us
    ppermute x15, waiting for transfers between devices, swapped(): return lax.ppermute(value, axis, pairs)  63.8 us
    all_gather x1, waiting for transfers between devices, body(): lax.all_gather(jnp.dot(upstream, right_two[0].T, preferred_element_type=j...  34.1 us
    unnamed x44, local copies, waits for them, and re-layouts  22.8 us
    ppermute x15, starting transfers between devices, swapped(): return lax.ppermute(value, axis, pairs)  15.9 us
    ppermute x1, waiting for transfers between devices, shifted(): lax.ppermute(shard, axis, [(i, (i + by) % peers) for i in range(peers)])  14.3 us
    reduce_sum x1, other arithmetic, body(): jnp.sum(lax.all_gather(jnp.dot(upstream, right_two[0].T, preferred_elemen...  12.8 us
    dot_general x1, matrix products, body(): jnp.einsum('ktcb,cjkeb->tcje', grad_view, second_view, preferred_element_...  8.47 us
  transfers between devices with their start and end apart: 17, of which 5 were waited for; matrix products, arithmetic and copies ran while one was open for 12% of the time, Pallas kernels for 0%

profile of v1, /device:TPU:6, one launch (start us, length us, event | category | flops | bytes accessed | tf_op | source)
XLA Modules:
  0.0 416.6 jit_solution(16099263809354757595)
XLA Ops:
  7.2 0.9 collective-permute-start
  8.1 14.3 %collective-permute-done = bf16[1024,256]{1,0:T(8,128)(2,1)S(1)} collective-permute-done((bf16[1024,256]{1,0:T(8,128)(2,1)}, bf16[1024,256]{1,0:T(8,128)(2,1)S(1)}, u32[]{:S(2)}, u32[]{:S(2)}) %collective-permute-start) | collective-permute-done | bytes 524320 | tf_op jit(solution)/shard_map/ppermute | solution.py:15
  22.4 0.8 copy-done.5
  23.2 2.2 fusion.67
  25.4 4.0 collective-permute-start.15
  29.4 1.0 collective-permute-start.14
  30.4 3.2 collective-permute-start.13
  33.6 0.7 collective-permute-start.12
  34.3 3.9 copy.16
  38.2 2.4 fusion.17
  40.6 1.7 fusion.33
  42.4 1.3 fusion.64
  43.8 1.3 collective-permute-start.5
  45.0 1.1 bitcast_dynamic-update-slice_fusion.4
  46.1 26.8 %collective-permute-done.12 = bf16[1024,256]{1,0:T(8,128)(2,1)} collective-permute-done((bf16[1024,256]{1,0:T(8,128)(2,1)}, bf16[1024,256]{1,0:T(8,128)(2,1)}, u32[]{:S(2)}, u32[]{:S(2)}) %collective-permute-start.12) | collective-permute-done | bytes 524320 | tf_op jit(solution)/shard_map/ppermute | solution.py:10
  72.9 1.0 collective-permute-start.4
  73.9 1.1 bitcast_dynamic-update-slice_fusion.3
  75.1 1.1 bitcast_dynamic-update-slice_fusion.2
  76.2 1.4 collective-permute-start.2
  77.6 1.1 bitcast_dynamic-update-slice_fusion.1
  78.7 0.3 collective-permute-start.3
  79.0 1.1 bitcast_dynamic-update-slice_fusion
  80.1 15.3 %collective-permute-done.2 = bf16[1024,256]{1,0:T(8,128)(2,1)S(1)} collective-permute-done((bf16[1024,256]{1,0:T(8,128)(2,1)S(1)}, bf16[1024,256]{1,0:T(8,128)(2,1)S(1)}, u32[]{:S(2)}, u32[]{:S(2)}) %collective-permute-start.2) | collective-permute-done | bytes 524320 | tf_op jit(solution)/shard_map/ppermute | solution.py:10
  95.5 21.6 %collective-permute-done.3 = bf16[1024,256]{1,0:T(8,128)(2,1)S(1)} collective-permute-done((bf16[1024,256]{1,0:T(8,128)(2,1)S(1)}, bf16[1024,256]{1,0:T(8,128)(2,1)S(1)}, u32[]{:S(2)}, u32[]{:S(2)}) %collective-permute-start.3) | collective-permute-done | bytes 524320 | tf_op jit(solution)/shard_map/ppermute | solution.py:10
  117.3 1.7 copy-done.11
  119.0 4.9 %convert_bitcast_fusion.1 = bf16[1,4,6,256,256]{3,4,1,2,0:T(8,128)(2,1)} fusion(bf16[1024,4,256,1]{0,2,1,3:T(8,128)(2,1)S(1)} %bitcast.209, bf16[6,1024,256]{2,1,0:T(8,128)(2,1)S(1)} %bitcast_dynamic-update-slice_fusion.5), kind=kOutput, calls=%fused_computation.31 | convolution fusion | flops 3222798336 | bytes 8388608 | tf_op jit(solution)/shard_map/tcje,ktcb->cjkeb/dot_general | solution.py:104
  123.9 4.7 %copy.27 = bf16[1,4,6,256,256]{4,3,2,1,0:T(8,128)(2,1)} copy(bf16[1,4,6,256,256]{3,4,1,2,0:T(8,128)(2,1)} %convert_bitcast_fusion.1) | data formatting | bytes 6291456
  128.5 8.5 %fusion.24 = f32[1024,4,256,1]{0,2,3,1:T(8,128)} fusion(bf16[1,4,6,256,256]{4,3,2,1,0:T(8,128)(2,1)} %param.13, bf16[6,1024,256]{2,1,0:T(8,128)(2,1)} %copy-done.11), kind=kOutput, calls=%fused_computation.28 | convolution fusion | flops 3221225472 | bytes 10485760 | tf_op jit(solution)/shard_map/ktcb,cjkeb->tcje/dot_general | solution.py:76
  137.0 34.1 %all-gather.3.cloned.1.call-done = f32[32768,256]{1,0:T(8,128)} async-done(((f32[1024,256]{1,0:T(8,128)}), f32[32768,256]{1,0:T(8,128)}) %all-gather.3.cloned.1.call-update) | async-done | bytes 33554448 | tf_op jit(solution)/shard_map/all_gather | solution.py:69
  171.0 12.8 %reduce_sum.9 = bf16[1024,256]{1,0:T(8,128)(2,1)} reduce(f32[32,1024,256]{2,1,0:T(8,128)} %bitcast.203, f32[]{:T(128)} %constant.0.clone.1), dimensions={0}, to_apply=%region_0.0 | reduce | flops 8126464 | bytes 34078724 | tf_op jit(solution)/shard_map/reduce_sum | solution.py:68
  183.8 4.7 %fusion.12 = bf16[1024,1024]{0,1:T(8,128)(2,1)S(1)} fusion(bf16[1,1024,1024]{1,2,0:T(8,128)(2,1)} %copy.16, f32[1024,4,256,1]{0,2,3,1:T(8,128)} %fusion.24, bf16[1,1024,256]{2,1,0:T(8,128)(2,1)} %param.16, bf16[1024,256]{1,0:T(8,128)(2,1)} %reduce_sum.9), kind=kOutput, calls=%fused_computation.15 | convolution fusion | flops 549453824 | bytes 9437184 | tf_op jit(solution)/shard_map/dot_general | solution.py:79
  188.6 1.8 fusion.51
  190.3 1.3 copy-done.13
  191.6 4.9 %convert_bitcast_fusion.2 = bf16[1,4,6,256,256]{3,4,2,1,0:T(8,128)(2,1)} fusion(bf16[1024,4,256,1]{0,2,3,1:T(8,128)(2,1)S(1)} %bitcast.207, bf16[6,1024,256]{2,1,0:T(8,128)(2,1)S(1)} %copy-done.13), kind=kOutput, calls=%fused_computation.32 | convolution fusion | flops 3222798336 | bytes 8388608 | tf_op jit(solution)/shard_map/ktcb,tcje->cjkbe/dot_general | solution.py:97
  196.5 3.5 fusion.22
  200.0 1.2 slice_bitcast_fusion
  201.2 2.6 slice_bitcast_fusion.4
  203.8 0.5 copy-done.2
  204.6 1.0 collective-permute-start.9
  205.6 1.7 collective-permute-start.8
  207.4 183.6 %all-reduce.2 = (bf16[1024,256]{1,0:T(8,128)(2,1)}, bf16[1024,256]{1,0:T(8,128)(2,1)}, bf16[1024,256]{1,0:T(8,128)(2,1)}) all-reduce(f32[1024,256]{1,0:T(8,128)} %fusion.51, f32[1024,256]{1,0:T(8,128)} %fusion.64, f32[1024,256]{1,0:T(8,128)} %fusion.33), channel_id=1, replica_groups=mesh['section'=4,'tensor'=32] {'tensor'}, use_global_device_ids=true, to_apply=%region_1.0 | all-reduce | flops 786432 | bytes 4718592 | tf_op jit(solution)/shard_map/psum | solution.py:81
  391.0 1.5 fusion.49
  392.5 0.8 copy.28
  393.3 4.6 %copy.26 = bf16[1,4,6,256,256]{4,3,2,1,0:T(8,128)(2,1)} copy(bf16[1,4,6,256,256]{3,4,2,1,0:T(8,128)(2,1)} %convert_bitcast_fusion.2) | data formatting | bytes 6291456
  397.9 2.4 fusion.50
  400.3 3.3 fusion.44
  403.6 2.0 fusion.45
  405.6 4.1 fusion.48
  (52 shorter events, 0.8 us)
Async XLA Ops:
  7.2 189.3 %copy-start = (bf16[1,4,6,256,256]{4,3,2,1,0:T(8,128)(2,1)S(1)}, bf16[1,4,6,256,256]{4,3,2,1,0:T(8,128)(2,1)}, u32[]{:S(2)}) copy-start(bf16[1,4,6,256,256]{4,3,2,1,0:T(8,128)(2,1)} %param.12) | copy-start | bytes 9437188
  7.2 163.9 %all-gather.3.cloned.1.call-start = ((), (), s32[]{:S(2)}) async-start(), calls=%async_computation | async-start | bytes 34603008 | tf_op jit(solution)/shard_map/all_gather | solution.py:69
  7.2 15.2 %collective-permute-start = (bf16[1024,256]{1,0:T(8,128)(2,1)}, bf16[1024,256]{1,0:T(8,128)(2,1)S(1)}, u32[]{:S(2)}, u32[]{:S(2)}) collective-permute-start(bf16[1024,256]{1,0:T(8,128)(2,1)} %bitcast.215), channel_id=1, source_target_pairs={{0,96},{32,0},{64,32},{96,64},{1,97},{33,1},{65,33},{97,65},{2,98}... | collective-permute-start | bytes 1572872 | tf_op jit(solution)/shard_map/ppermute | solution.py:15
  22.4 0.8 copy-start.5
  25.4 53.3 %collective-permute-start.15 = (bf16[1024,256]{1,0:T(8,128)(2,1)}, bf16[1024,256]{1,0:T(8,128)(2,1)}, u32[]{:S(2)}, u32[]{:S(2)}) collective-permute-start(bf16[1024,256]{1,0:T(8,128)(2,1)} %bitcast.210), channel_id=1, source_target_pairs={{0,16},{1,17},{2,18},{3,19},{4,20},{5,21},{6,22},{7,23},{8,24},{9,... | collective-permute-start | bytes 1572872 | tf_op jit(solution)/shard_map/ppermute | solution.py:10
  29.4 46.8 %collective-permute-start.14 = (bf16[1024,256]{1,0:T(8,128)(2,1)}, bf16[1024,256]{1,0:T(8,128)(2,1)}, u32[]{:S(2)}, u32[]{:S(2)}) collective-permute-start(bf16[1024,256]{1,0:T(8,128)(2,1)} %bitcast.211), channel_id=1, source_target_pairs={{0,8},{1,9},{2,10},{3,11},{4,12},{5,13},{6,14},{7,15},{8,0},{9,1},... | collective-permute-start | bytes 1572872 | tf_op jit(solution)/shard_map/ppermute | solution.py:10
  30.4 44.6 %collective-permute-start.13 = (bf16[1024,256]{1,0:T(8,128)(2,1)}, bf16[1024,256]{1,0:T(8,128)(2,1)}, u32[]{:S(2)}, u32[]{:S(2)}) collective-permute-start(bf16[1024,256]{1,0:T(8,128)(2,1)} %bitcast.212), channel_id=1, source_target_pairs={{0,4},{1,5},{2,6},{3,7},{4,0},{5,1},{6,2},{7,3},{8,12},{9,13},{10,... | collective-permute-start | bytes 1572872 | tf_op jit(solution)/shard_map/ppermute | solution.py:10
  33.6 39.3 %collective-permute-start.12 = (bf16[1024,256]{1,0:T(8,128)(2,1)}, bf16[1024,256]{1,0:T(8,128)(2,1)}, u32[]{:S(2)}, u32[]{:S(2)}) collective-permute-start(bf16[1024,256]{1,0:T(8,128)(2,1)} %bitcast.213), channel_id=1, source_target_pairs={{0,2},{1,3},{2,0},{3,1},{4,6},{5,7},{6,4},{7,5},{8,10},{9,11},{10,... | collective-permute-start | bytes 1572872 | tf_op jit(solution)/shard_map/ppermute | solution.py:10
  34.3 9.5 %collective-permute-start.11 = (bf16[1024,256]{1,0:T(8,128)(2,1)}, bf16[1024,256]{1,0:T(8,128)(2,1)}, u32[]{:S(2)}, u32[]{:S(2)}) collective-permute-start(bf16[1024,256]{1,0:T(8,128)(2,1)} %bitcast.214), channel_id=1, source_target_pairs={{0,1},{1,0},{2,3},{3,2},{4,5},{5,4},{6,7},{7,6},{8,9},{9,8},{10,11... | collective-permute-start | bytes 1572872 | tf_op jit(solution)/shard_map/ppermute | solution.py:10
  38.2 2.4 copy-start.14
  40.6 1.7 copy-start.4
  40.6 1.7 copy-start.9
  40.6 3.1 copy-start.6
  43.8 73.5 %collective-permute-start.5 = (bf16[1024,256]{1,0:T(8,128)(2,1)S(1)}, bf16[1024,256]{1,0:T(8,128)(2,1)S(1)}, u32[]{:S(2)}, u32[]{:S(2)}) collective-permute-start(bf16[1024,256]{1,0:T(8,128)(2,1)S(1)} %copy-done.6), channel_id=1, source_target_pairs={{0,16},{1,17},{2,18},{3,19},{4,20},{5,21},{6,22},{7,23},{8,24},{9,... | collective-permute-start | bytes 1572872 | tf_op jit(solution)/shard_map/ppermute | solution.py:10
  72.9 44.3 %collective-permute-start.4 = (bf16[1024,256]{1,0:T(8,128)(2,1)S(1)}, bf16[1024,256]{1,0:T(8,128)(2,1)S(1)}, u32[]{:S(2)}, u32[]{:S(2)}) collective-permute-start(bf16[1024,256]{1,0:T(8,128)(2,1)S(1)} %copy-done.6), channel_id=1, source_target_pairs={{0,8},{1,9},{2,10},{3,11},{4,12},{5,13},{6,14},{7,15},{8,0},{9,1},... | collective-permute-start | bytes 1572872 | tf_op jit(solution)/shard_map/ppermute | solution.py:10
  75.0 5.1 %collective-permute-start.1 = (bf16[1024,256]{1,0:T(8,128)(2,1)S(1)}, bf16[1024,256]{1,0:T(8,128)(2,1)S(1)}, u32[]{:S(2)}, u32[]{:S(2)}) collective-permute-start(bf16[1024,256]{1,0:T(8,128)(2,1)S(1)} %copy-done.6), channel_id=1, source_target_pairs={{0,1},{1,0},{2,3},{3,2},{4,5},{5,4},{6,7},{7,6},{8,9},{9,8},{10,11... | collective-permute-start | bytes 1572872 | tf_op jit(solution)/shard_map/ppermute | solution.py:10
  76.2 19.3 %collective-permute-start.2 = (bf16[1024,256]{1,0:T(8,128)(2,1)S(1)}, bf16[1024,256]{1,0:T(8,128)(2,1)S(1)}, u32[]{:S(2)}, u32[]{:S(2)}) collective-permute-start(bf16[1024,256]{1,0:T(8,128)(2,1)S(1)} %copy-done.6), channel_id=1, source_target_pairs={{0,2},{1,3},{2,0},{3,1},{4,6},{5,7},{6,4},{7,5},{8,10},{9,11},{10,... | collective-permute-start | bytes 1572872 | tf_op jit(solution)/shard_map/ppermute | solution.py:10
  78.7 38.4 %collective-permute-start.3 = (bf16[1024,256]{1,0:T(8,128)(2,1)S(1)}, bf16[1024,256]{1,0:T(8,128)(2,1)S(1)}, u32[]{:S(2)}, u32[]{:S(2)}) collective-permute-start(bf16[1024,256]{1,0:T(8,128)(2,1)S(1)} %copy-done.6), channel_id=1, source_target_pairs={{0,4},{1,5},{2,6},{3,7},{4,0},{5,1},{6,2},{7,3},{8,12},{9,13},{10,... | collective-permute-start | bytes 1572872 | tf_op jit(solution)/shard_map/ppermute | solution.py:10
  80.0 37.2 %copy-start.12 = (bf16[6,1024,256]{2,1,0:T(8,128)(2,1)}, bf16[6,1024,256]{2,1,0:T(8,128)(2,1)S(1)}, u32[]{:S(2)}) copy-start(bf16[6,1024,256]{2,1,0:T(8,128)(2,1)S(1)} %bitcast_dynamic-update-slice_fusion) | copy-start | bytes 9437188
  117.3 1.7 copy-start.11
  183.8 4.7 %copy-start.10 = (bf16[1,256,1024]{2,1,0:T(8,128)(2,1)S(1)}, bf16[1,256,1024]{2,1,0:T(8,128)(2,1)}, u32[]{:S(2)}) copy-start(bf16[1,256,1024]{2,1,0:T(8,128)(2,1)} %param.15) | copy-start | bytes 1572868
  188.6 7.9 %copy-start.3 = (bf16[1024,1024]{0,1:T(8,128)(2,1)}, bf16[1024,1024]{0,1:T(8,128)(2,1)S(1)}, u32[]{:S(2)}) copy-start(bf16[1024,1024]{0,1:T(8,128)(2,1)S(1)} %fusion.12) | copy-start | bytes 6291460
  188.6 3.0 copy-start.13
  200.0 4.3 %copy-start.2 = (f32[1024,6,256,1]{2,0,1,3:T(8,128)}, f32[1024,6,256,1]{2,0,1,3:T(8,128)S(1)}, u32[]{:S(2)}) copy-start(f32[1024,6,256,1]{2,0,1,3:T(8,128)S(1)} %fusion.22) | copy-start | bytes 18874372
  201.2 204.4 %collective-permute-start.10 = (f32[1024,256]{1,0:T(8,128)}, f32[1024,256]{1,0:T(8,128)}, u32[]{:S(2)}, u32[]{:S(2)}) collective-permute-start(f32[1024,256]{1,0:T(8,128)} %slice_bitcast_fusion), channel_id=1, source_target_pairs={{0,16},{1,17},{2,18},{3,19},{4,20},{5,21},{6,22},{7,23},{8,24},{9,... | collective-permute-start | bytes 3145736 | tf_op jit(solution)/shard_map/ppermute | solution.py:10
  204.3 201.3 %collective-permute-start.6 = (f32[1024,256]{1,0:T(8,128)}, f32[1024,256]{1,0:T(8,128)}, u32[]{:S(2)}, u32[]{:S(2)}) collective-permute-start(f32[1024,256]{1,0:T(8,128)} %get-tuple-element.17), channel_id=1, source_target_pairs={{0,1},{1,0},{2,3},{3,2},{4,5},{5,4},{6,7},{7,6},{8,9},{9,8},{10,11... | collective-permute-start | bytes 3145736 | tf_op jit(solution)/shard_map/ppermute | solution.py:10
  204.6 201.0 %collective-permute-start.9 = (f32[1024,256]{1,0:T(8,128)}, f32[1024,256]{1,0:T(8,128)}, u32[]{:S(2)}, u32[]{:S(2)}) collective-permute-start(f32[1024,256]{1,0:T(8,128)} %get-tuple-element.18), channel_id=1, source_target_pairs={{0,8},{1,9},{2,10},{3,11},{4,12},{5,13},{6,14},{7,15},{8,0},{9,1},... | collective-permute-start | bytes 3145736 | tf_op jit(solution)/shard_map/ppermute | solution.py:10
  205.6 200.0 %collective-permute-start.8 = (f32[1024,256]{1,0:T(8,128)}, f32[1024,256]{1,0:T(8,128)}, u32[]{:S(2)}, u32[]{:S(2)}) collective-permute-start(f32[1024,256]{1,0:T(8,128)} %get-tuple-element.19), channel_id=1, source_target_pairs={{0,4},{1,5},{2,6},{3,7},{4,0},{5,1},{6,2},{7,3},{8,12},{9,13},{10,... | collective-permute-start | bytes 3145736 | tf_op jit(solution)/shard_map/ppermute | solution.py:10
  207.3 198.3 %collective-permute-start.7 = (f32[1024,256]{1,0:T(8,128)}, f32[1024,256]{1,0:T(8,128)}, u32[]{:S(2)}, u32[]{:S(2)}) collective-permute-start(f32[1024,256]{1,0:T(8,128)} %get-tuple-element.20), channel_id=1, source_target_pairs={{0,2},{1,3},{2,0},{3,1},{4,6},{5,7},{6,4},{7,5},{8,10},{9,11},{10,... | collective-permute-start | bytes 3145736 | tf_op jit(solution)/shard_map/ppermute | solution.py:10
  397.9 5.7 %copy-start.1 = (bf16[1,1024,1024]{1,2,0:T(8,128)(2,1)S(1)}, bf16[1,1024,1024]{1,2,0:T(8,128)(2,1)}, u32[]{:S(2)}) copy-start(bf16[1,1024,1024]{1,2,0:T(8,128)(2,1)} %copy.16) | copy-start | bytes 6291460
  397.9 5.7 %copy-start.7 = (bf16[1024,256]{1,0:T(8,128)(2,1)S(1)}, bf16[1024,256]{1,0:T(8,128)(2,1)}, u32[]{:S(2)}) copy-start(bf16[1024,256]{1,0:T(8,128)(2,1)} %reduce_sum.9) | copy-start | bytes 1572868
  403.6 2.0 copy-start.8
Sparse Core Ops, SparseCore 0:
  25.5 145.4 all-gather.2
